TPU v7x, 128 devices: a whole 4x4x4 slice. The times are simulated.
128 devices in a mesh: row: 16 (over z_hi, y, core), col: 8 (over z_lo, x).
Axes of the slice: x: 4, y: 4, z: 4 (z_hi: 2, z_lo: 2; z = z_hi * 2 + z_lo), core: 2. Of those that a mesh axis runs over, the one named last changes fastest.
Arguments:
- grad_out: bfloat16 [262144, 256], P(('row', 'col')), may hold values from -6 to 6
- preact: bfloat16 [262144, 256], P(('row', 'col')), may hold values from -6 to 6
- features: bfloat16 [262144, 256], P(('col', 'row')), may hold values from -6 to 6
- weight: bfloat16 [256, 256], replicated, may hold values from -0.375 to 0.375
- tiles: bfloat16 [16, 8, 320, 128, 128], P('row', 'col'), may hold values from -0.099609375 to 0.099609375
- tile_rows: int32 [16, 8, 320], P('row', 'col'), may hold values from 0 to 127
- tile_cols: int32 [16, 8, 320], P('row', 'col'), may hold values from 0 to 255
- live_counts: int32 [16, 8], P('row', 'col'), may hold values from 80 to 320, as said below
Outputs:
- grad_features: bfloat16 [262144, 256], P(('col', 'row'))
- grad_weight: float32 [256, 256], replicated
Inputs may be any that keep to these rules, and one draw needn't show every extreme that they name: `live_counts`: some block holds exactly 320 live tiles in every draw.
All inputs are finite; a program needn't handle non-finite values.
Results may differ from a plain program's by a relative error of at most 0.02.
Values may be sent and summed in bfloat16 or wider, within the bound.
A program may use at most 192 MiB of HBM per device.

v0:
```python
import math
import jax
import jax.numpy as jnp
from jax import lax
from jax.sharding import PartitionSpec as P


def body(grad_out, preact, features, weight, tiles, tile_rows, tile_cols, live_counts):
    width = grad_out.shape[1]
    masked = jnp.where(preact > 0, grad_out, jnp.zeros_like(grad_out))
    block = lax.all_gather(masked, "col", axis=0, tiled=True)
    row_count = block.shape[0] // 128
    row_flat = block.reshape(row_count, 128 * width)
    slots = tiles.shape[2]
    tile_stack = tiles.reshape(slots, 128, 128)
    row_index = tile_rows.reshape(slots)
    col_index = tile_cols.reshape(slots)
    count = live_counts.reshape(())
    col_tiles = lax.axis_size("row") * grad_out.shape[0] // 128
    group = math.gcd(slots, 32)
    offsets = jnp.arange(group, dtype=jnp.int32)
    row_ids = jnp.arange(row_count, dtype=jnp.int32)
    col_ids = jnp.arange(col_tiles, dtype=jnp.int32)

    def add_group(step, accum):
        start = step * group
        tile_blk = lax.dynamic_slice_in_dim(tile_stack, start, group, 0)
        rows_now = lax.dynamic_slice_in_dim(row_index, start, group, 0)
        cols_now = lax.dynamic_slice_in_dim(col_index, start, group, 0) - 0
        pick = (rows_now[:, None] == row_ids[None, :]).astype(jnp.bfloat16)
        gathered = jnp.dot(pick, row_flat, preferred_element_type=jnp.float32).astype(jnp.bfloat16)
        gathered = gathered.reshape(group, 128, width)
        prod = jnp.einsum("kab,kaf->kbf", tile_blk, gathered, preferred_element_type=jnp.float32)
        upper = prod.astype(jnp.bfloat16)
        lower = (prod - upper.astype(jnp.float32)).astype(jnp.bfloat16)
        keep = start + offsets < count
        place = ((cols_now[None, :] == col_ids[:, None]) & keep[None, :]).astype(jnp.bfloat16)
        both_place = jnp.concatenate([place, place], axis=1)
        both_vals = jnp.concatenate([upper, lower], axis=0).reshape(2 * group, 128 * width)
        return accum + jnp.dot(both_place, both_vals, preferred_element_type=jnp.float32)

    accum = jnp.zeros((col_tiles, 128 * width), jnp.float32)
    accum = lax.fori_loop(0, slots // group, add_group, accum)
    partial_value = accum.reshape(col_tiles * 128, width)
    summed = lax.psum_scatter(
        partial_value.astype(jnp.bfloat16), "row", scatter_dimension=0, tiled=True
    )
    grad_features = lax.dot_general(
        summed, weight, (((1,), (1,)), ((), ())), preferred_element_type=jnp.float32
    ).astype(jnp.bfloat16)
    weight_term = lax.dot_general(
        features, summed, (((0,), (0,)), ((), ())), preferred_element_type=jnp.float32
    )
    grad_weight = lax.psum(weight_term, ("row", "col"))
    return (grad_features, grad_weight)


def solution(mesh):
    in_specs = (
        P(("row", "col"), None),
        P(("row", "col"), None),
        P(("col", "row"), None),
        P(),
        P("row", "col", None, None, None),
        P("row", "col", None),
        P("row", "col", None),
        P("row", "col"),
    )
    out_specs = (P(("col", "row"), None), P())
    return jax.shard_map(body, mesh=mesh, in_specs=in_specs, out_specs=out_specs, check_vma=False)
```

profile of v0, /device:TPU:1, one launch (start us, length us, event | category | flops | bytes accessed | tf_op | source)
XLA Modules:
  0.0 803.8 jit_solution(6973166508205975980)
XLA Ops:
  10.1 14.5 %copy.12 = bf16[1,1,320,128,128]{3,4,2,1,0:T(8,128)(2,1)} copy(bf16[1,1,320,128,128]{4,3,2,1,0:T(8,128)(2,1)} %param.14) | data formatting | bytes 20971520 | tf_op args[4]
  24.6 80.9 %all-gather.2.cloned.1.call-done = bf16[16384,256]{1,0:T(8,128)(2,1)} async-done(((bf16[2048,256]{1,0:T(8,128)(2,1)}), bf16[16384,256]{1,0:T(8,128)(2,1)}) %all-gather.2.cloned.1.call-update) | async-done | bytes 8388624 | tf_op jit(solution)/shard_map/all_gather | solution.py:11
  105.4 13.4 %reshape.49 = bf16[128,32768]{1,0:T(8,128)(2,1)} reshape(bf16[16384,256]{1,0:T(8,128)(2,1)} %all-gather.2.cloned.1.call-done) | data formatting | bytes 16777216 | tf_op jit(solution)/shard_map/reshape | solution.py:13
  118.9 342.9 %while.14 = (s32[]{:T(128)}, f32[256,32768]{1,0:T(8,128)}, s32[320]{0:T(512)S(1)}, s32[]{:T(128)}, bf16[320,128,128]{1,2,0:T(8,128)(2,1)}, /*index=5*/s32[320]{0...) while((s32[]{:T(128)}, f32[256,32768]{1,0:T(8,128)}, ...), condition=%wide.region_1.2_spmd.clone, body=%wide.region_0.1_spmd.clone.sunk | while | flops 1634766848 | bytes 110117888 | solution.py:43
  129.8 12.4 %convolution_add_fusion.2 = f32[256,32768]{1,0:T(8,128)} fusion(bf16[64,32768]{1,0:T(8,128)(2,1)S(1)} %bitcast.29, f32[256,32768]{1,0:T(8,128)} %get-tuple-element.281, pred[]{:T(512)S(6)} %compare.3, pred[256,32]{0,1:T(32,128)(4,1)S(1)} %fusion.34), kind=kOutput, calls=%fused_computation.3.clone.1 | convolution fusion | flops 1090535424 | bytes 71311360 | tf_op jit(solution)/shard_map/while/body/eval_jaxpr/dot_general | solution.py:40
  143.2 4.6 convolution_convert_fusion.3
  153.2 24.6 %convolution_add_fusion.2 = f32[256,32768]{1,0:T(8,128)} fusion(bf16[64,32768]{1,0:T(8,128)(2,1)S(1)} %bitcast.29, f32[256,32768]{1,0:T(8,128)} %get-tuple-element.281, pred[]{:T(512)S(6)} %compare.3, pred[256,32]{0,1:T(32,128)(4,1)S(1)} %fusion.34), kind=kOutput, calls=%fused_computation.3.clone.1 | convolution fusion | flops 1090535424 | bytes 71311360 | tf_op jit(solution)/shard_map/while/body/eval_jaxpr/dot_general | solution.py:40
  178.7 4.6 convolution_convert_fusion.3
  188.7 24.6 %convolution_add_fusion.2 = f32[256,32768]{1,0:T(8,128)} fusion(bf16[64,32768]{1,0:T(8,128)(2,1)S(1)} %bitcast.29, f32[256,32768]{1,0:T(8,128)} %get-tuple-element.281, pred[]{:T(512)S(6)} %compare.3, pred[256,32]{0,1:T(32,128)(4,1)S(1)} %fusion.34), kind=kOutput, calls=%fused_computation.3.clone.1 | convolution fusion | flops 1090535424 | bytes 71311360 | tf_op jit(solution)/shard_map/while/body/eval_jaxpr/dot_general | solution.py:40
  214.2 4.6 convolution_convert_fusion.3
  224.2 24.6 %convolution_add_fusion.2 = f32[256,32768]{1,0:T(8,128)} fusion(bf16[64,32768]{1,0:T(8,128)(2,1)S(1)} %bitcast.29, f32[256,32768]{1,0:T(8,128)} %get-tuple-element.281, pred[]{:T(512)S(6)} %compare.3, pred[256,32]{0,1:T(32,128)(4,1)S(1)} %fusion.34), kind=kOutput, calls=%fused_computation.3.clone.1 | convolution fusion | flops 1090535424 | bytes 71311360 | tf_op jit(solution)/shard_map/while/body/eval_jaxpr/dot_general | solution.py:40
  249.7 4.6 convolution_convert_fusion.3
  259.7 24.6 %convolution_add_fusion.2 = f32[256,32768]{1,0:T(8,128)} fusion(bf16[64,32768]{1,0:T(8,128)(2,1)S(1)} %bitcast.29, f32[256,32768]{1,0:T(8,128)} %get-tuple-element.281, pred[]{:T(512)S(6)} %compare.3, pred[256,32]{0,1:T(32,128)(4,1)S(1)} %fusion.34), kind=kOutput, calls=%fused_computation.3.clone.1 | convolution fusion | flops 1090535424 | bytes 71311360 | tf_op jit(solution)/shard_map/while/body/eval_jaxpr/dot_general | solution.py:40
  295.2 24.6 %convolution_add_fusion.2 = f32[256,32768]{1,0:T(8,128)} fusion(bf16[64,32768]{1,0:T(8,128)(2,1)S(1)} %bitcast.29, f32[256,32768]{1,0:T(8,128)} %get-tuple-element.281, pred[]{:T(512)S(6)} %compare.3, pred[256,32]{0,1:T(32,128)(4,1)S(1)} %fusion.34), kind=kOutput, calls=%fused_computation.3.clone.1 | convolution fusion | flops 1090535424 | bytes 71311360 | tf_op jit(solution)/shard_map/while/body/eval_jaxpr/dot_general | solution.py:40
  330.7 24.6 %convolution_add_fusion.2 = f32[256,32768]{1,0:T(8,128)} fusion(bf16[64,32768]{1,0:T(8,128)(2,1)S(1)} %bitcast.29, f32[256,32768]{1,0:T(8,128)} %get-tuple-element.281, pred[]{:T(512)S(6)} %compare.3, pred[256,32]{0,1:T(32,128)(4,1)S(1)} %fusion.34), kind=kOutput, calls=%fused_computation.3.clone.1 | convolution fusion | flops 1090535424 | bytes 71311360 | tf_op jit(solution)/shard_map/while/body/eval_jaxpr/dot_general | solution.py:40
  366.2 24.6 %convolution_add_fusion.2 = f32[256,32768]{1,0:T(8,128)} fusion(bf16[64,32768]{1,0:T(8,128)(2,1)S(1)} %bitcast.29, f32[256,32768]{1,0:T(8,128)} %get-tuple-element.281, pred[]{:T(512)S(6)} %compare.3, pred[256,32]{0,1:T(32,128)(4,1)S(1)} %fusion.34), kind=kOutput, calls=%fused_computation.3.clone.1 | convolution fusion | flops 1090535424 | bytes 71311360 | tf_op jit(solution)/shard_map/while/body/eval_jaxpr/dot_general | solution.py:40
  391.7 4.6 convolution_convert_fusion.3
  401.7 24.6 %convolution_add_fusion.2 = f32[256,32768]{1,0:T(8,128)} fusion(bf16[64,32768]{1,0:T(8,128)(2,1)S(1)} %bitcast.29, f32[256,32768]{1,0:T(8,128)} %get-tuple-element.281, pred[]{:T(512)S(6)} %compare.3, pred[256,32]{0,1:T(32,128)(4,1)S(1)} %fusion.34), kind=kOutput, calls=%fused_computation.3.clone.1 | convolution fusion | flops 1090535424 | bytes 71311360 | tf_op jit(solution)/shard_map/while/body/eval_jaxpr/dot_general | solution.py:40
  427.2 4.6 convolution_convert_fusion.3
  437.2 24.6 %convolution_add_fusion.2 = f32[256,32768]{1,0:T(8,128)} fusion(bf16[64,32768]{1,0:T(8,128)(2,1)S(1)} %bitcast.29, f32[256,32768]{1,0:T(8,128)} %get-tuple-element.281, pred[]{:T(512)S(6)} %compare.3, pred[256,32]{0,1:T(32,128)(4,1)S(1)} %fusion.34), kind=kOutput, calls=%fused_computation.3.clone.1 | convolution fusion | flops 1090535424 | bytes 71311360 | tf_op jit(solution)/shard_map/while/body/eval_jaxpr/dot_general | solution.py:40
  461.8 17.1 %convert_element_type.45 = bf16[256,32768]{1,0:T(8,128)(2,1)} convert(f32[256,32768]{1,0:T(8,128)} %get-tuple-element.171) | non-fusion elementwise | flops 8388608 | bytes 50331648 | tf_op jit(solution)/shard_map/convert_element_type | solution.py:46
  478.9 25.6 %convert_element_type.46 = bf16[32768,256]{1,0:T(8,128)(2,1)} reshape(bf16[256,32768]{1,0:T(8,128)(2,1)} %convert_element_type.45) | data formatting | bytes 33554432 | tf_op jit(solution)/shard_map/convert_element_type | solution.py:46
  504.6 145.1 %reduce-scatter.2.cloned.1.call-done = bf16[2048,256]{1,0:T(8,128)(2,1)} async-done(((bf16[32768,256]{1,0:T(8,128)(2,1)}), bf16[2048,256]{1,0:T(8,128)(2,1)}) %reduce-scatter.2.cloned.1.call-update) | async-done | bytes 1048592 | tf_op jit(solution)/shard_map/reduce_scatter | solution.py:45
  654.8 140.8 %all-reduce.2.cloned.1.call-done = f32[256,256]{0,1:T(8,128)} async-done(((f32[256,256]{0,1:T(8,128)}), f32[256,256]{0,1:T(8,128)}) %all-reduce.2.cloned.1.call-update) | async-done | bytes 262160 | tf_op jit(solution)/shard_map/psum | solution.py:54
  (105 shorter events, 90.7 us)
Async XLA Ops:
  7.2 642.5 %copy-start = (bf16[2048,256]{1,0:T(8,128)(2,1)S(1)}, bf16[2048,256]{1,0:T(8,128)(2,1)}, u32[]{:S(2)}) copy-start(bf16[2048,256]{1,0:T(8,128)(2,1)} %param.12) | copy-start | bytes 3145732
  7.2 2.9 copy-start.2
  7.2 2.9 copy-start.3
  7.2 98.2 %all-gather.2.cloned.1.call-start = ((), (), s32[]{:S(2)}) async-start(), calls=%async_computation.1 | async-start | bytes 9437184 | tf_op jit(solution)/shard_map/all_gather | solution.py:11
  10.0 639.7 %reduce-scatter.2.cloned.1.call-start = ((), (), s32[]{:S(2)}) async-start(), calls=%async_computation.2 | async-start | bytes 17825792 | tf_op jit(solution)/shard_map/reduce_scatter | solution.py:45
  504.5 147.6 %copy-start.1 = (bf16[256,256]{1,0:T(8,128)(2,1)S(1)}, bf16[256,256]{1,0:T(8,128)(2,1)}, u32[]{:S(2)}) copy-start(bf16[256,256]{1,0:T(8,128)(2,1)} %param.13) | copy-start | bytes 393220
  504.6 291.0 %all-reduce.2.cloned.1.call-start = ((), (), s32[]{:S(2)}) async-start(), calls=%async_computation.3 | async-start | bytes 524288 | tf_op jit(solution)/shard_map/psum | solution.py:54
Sparse Core Ops, SparseCore 0:
  10.3 95.1 all-gather.1
  504.7 144.9 reduce-scatter.1
  655.7 139.7 all-reduce.1
where the time goes:
time: 806 us; the launch traced here: 804 us
  waiting for transfers between devices  367 us (46%)
  matrix products  304 us (38%)
  local copies, waits for them, and re-layouts  87.5 us (11%)
  other arithmetic  30.8 us (4%)
  between operations  13.8 us (2%)
    dot_general x10, matrix products, add_group(): jnp.dot(both_place, both_vals, preferred_element_type=jnp.float32)  234 us
    reduce_scatter x1, waiting for transfers between devices, body(): lax.psum_scatter(partial_value.astype(jnp.bfloat16), 'row', scatter_dimen...  145 us
    psum x1, waiting for transfers between devices, body(): grad_weight = lax.psum(weight_term, ('row', 'col'))  141 us
    all_gather x1, waiting for transfers between devices, body(): block = lax.all_gather(masked, 'col', axis=0, tiled=True)  80.9 us
    dot_general x10, matrix products, add_group(): jnp.dot(pick, row_flat, preferred_element_type=jnp.float32)  46.4 us
    while x20, local copies, waits for them, and re-layouts  30.6 us
    convert_element_type x1, local copies, waits for them, and re-layouts, body(): partial_value.astype(jnp.bfloat16)  25.6 us
    dot_general x10, matrix products, add_group(): jnp.einsum('kab,kaf->kbf', tile_blk, gathered, preferred_element_type=jnp...  19.4 us
  transfers between devices with their start and end apart: 3, of which 3 were waited for; matrix products, arithmetic and copies ran while one was open for 2% of the time, Pallas kernels for 0%

commit v1 on v0

--- a/solution.py
+++ b/solution.py
@@ -51,7 +51,7 @@
     weight_term = lax.dot_general(
         features, summed, (((0,), (0,)), ((), ())), preferred_element_type=jnp.float32
     )
-    grad_weight = lax.psum(weight_term, ("row", "col"))
+    grad_weight = lax.psum(lax.psum(weight_term, "row"), "col")
     return (grad_features, grad_weight)
 
 

time: 806 us -> 876 us (1.087)
  waiting for transfers between devices: 367 us -> 432 us
    psum x1 -> x2, waiting for transfers between devices: 141 us -> 206 us  [body(): grad_weight = lax.psum(lax.psum(weight_term, 'row'), 'col')]
  transfers between devices with their start and end apart: 3 -> 4, of which waited for: 3 -> 4; matrix products, arithmetic and copies ran while one was open for 2% -> 2% of each run, Pallas kernels for 0% -> 0%
where the time goes in v1:
time: 876 us; the launch traced here: 869 us
  waiting for transfers between devices  432 us (49%)
  matrix products  304 us (35%)
  local copies, waits for them, and re-layouts  87.5 us (10%)
  other arithmetic  30.8 us (4%)
  between operations  13.8 us (2%)
    dot_general x10, matrix products, add_group(): jnp.dot(both_place, both_vals, preferred_element_type=jnp.float32)  234 us
    psum x2, waiting for transfers between devices, body(): grad_weight = lax.psum(lax.psum(weight_term, 'row'), 'col')  206 us
    reduce_scatter x1, waiting for transfers between devices, body(): lax.psum_scatter(partial_value.astype(jnp.bfloat16), 'row', scatter_dimen...  145 us
    all_gather x1, waiting for transfers between devices, body(): block = lax.all_gather(masked, 'col', axis=0, tiled=True)  80.9 us
    dot_general x10, matrix products, add_group(): jnp.dot(pick, row_flat, preferred_element_type=jnp.float32)  46.4 us
    while x20, local copies, waits for them, and re-layouts  30.6 us
    convert_element_type x1, local copies, waits for them, and re-layouts, body(): partial_value.astype(jnp.bfloat16)  25.6 us
    dot_general x10, matrix products, add_group(): jnp.einsum('kab,kaf->kbf', tile_blk, gathered, preferred_element_type=jnp...  19.4 us
  transfers between devices with their start and end apart: 4, of which 4 were waited for; matrix products, arithmetic and copies ran while one was open for 2% of the time, Pallas kernels for 0%

profile of v1, /device:TPU:1, one launch (start us, length us, event | category | flops | bytes accessed | tf_op | source)
XLA Modules:
  0.0 869.4 jit_solution(1486265573028705820)
XLA Ops:
  10.1 14.5 %copy.12 = bf16[1,1,320,128,128]{3,4,2,1,0:T(8,128)(2,1)} copy(bf16[1,1,320,128,128]{4,3,2,1,0:T(8,128)(2,1)} %param.14) | data formatting | bytes 20971520 | tf_op args[4]
  24.6 80.9 %all-gather.2.cloned.1.call-done = bf16[16384,256]{1,0:T(8,128)(2,1)} async-done(((bf16[2048,256]{1,0:T(8,128)(2,1)}), bf16[16384,256]{1,0:T(8,128)(2,1)}) %all-gather.2.cloned.1.call-update) | async-done | bytes 8388624 | tf_op jit(solution)/shard_map/all_gather | solution.py:11
  105.4 13.4 %reshape.49 = bf16[128,32768]{1,0:T(8,128)(2,1)} reshape(bf16[16384,256]{1,0:T(8,128)(2,1)} %all-gather.2.cloned.1.call-done) | data formatting | bytes 16777216 | tf_op jit(solution)/shard_map/reshape | solution.py:13
  118.9 342.9 %while.14 = (s32[]{:T(128)}, f32[256,32768]{1,0:T(8,128)}, s32[320]{0:T(512)S(1)}, s32[]{:T(128)}, bf16[320,128,128]{1,2,0:T(8,128)(2,1)}, /*index=5*/s32[320]{0...) while((s32[]{:T(128)}, f32[256,32768]{1,0:T(8,128)}, ...), condition=%wide.region_1.2_spmd.clone, body=%wide.region_0.1_spmd.clone.sunk | while | flops 1634766848 | bytes 110117888 | solution.py:43
  129.8 12.4 %convolution_add_fusion.2 = f32[256,32768]{1,0:T(8,128)} fusion(bf16[64,32768]{1,0:T(8,128)(2,1)S(1)} %bitcast.29, f32[256,32768]{1,0:T(8,128)} %get-tuple-element.281, pred[]{:T(512)S(6)} %compare.3, pred[256,32]{0,1:T(32,128)(4,1)S(1)} %fusion.34), kind=kOutput, calls=%fused_computation.3.clone.1 | convolution fusion | flops 1090535424 | bytes 71311360 | tf_op jit(solution)/shard_map/while/body/eval_jaxpr/dot_general | solution.py:40
  143.2 4.6 convolution_convert_fusion.3
  153.2 24.6 %convolution_add_fusion.2 = f32[256,32768]{1,0:T(8,128)} fusion(bf16[64,32768]{1,0:T(8,128)(2,1)S(1)} %bitcast.29, f32[256,32768]{1,0:T(8,128)} %get-tuple-element.281, pred[]{:T(512)S(6)} %compare.3, pred[256,32]{0,1:T(32,128)(4,1)S(1)} %fusion.34), kind=kOutput, calls=%fused_computation.3.clone.1 | convolution fusion | flops 1090535424 | bytes 71311360 | tf_op jit(solution)/shard_map/while/body/eval_jaxpr/dot_general | solution.py:40
  178.7 4.6 convolution_convert_fusion.3
  188.7 24.6 %convolution_add_fusion.2 = f32[256,32768]{1,0:T(8,128)} fusion(bf16[64,32768]{1,0:T(8,128)(2,1)S(1)} %bitcast.29, f32[256,32768]{1,0:T(8,128)} %get-tuple-element.281, pred[]{:T(512)S(6)} %compare.3, pred[256,32]{0,1:T(32,128)(4,1)S(1)} %fusion.34), kind=kOutput, calls=%fused_computation.3.clone.1 | convolution fusion | flops 1090535424 | bytes 71311360 | tf_op jit(solution)/shard_map/while/body/eval_jaxpr/dot_general | solution.py:40
  214.2 4.6 convolution_convert_fusion.3
  224.2 24.6 %convolution_add_fusion.2 = f32[256,32768]{1,0:T(8,128)} fusion(bf16[64,32768]{1,0:T(8,128)(2,1)S(1)} %bitcast.29, f32[256,32768]{1,0:T(8,128)} %get-tuple-element.281, pred[]{:T(512)S(6)} %compare.3, pred[256,32]{0,1:T(32,128)(4,1)S(1)} %fusion.34), kind=kOutput, calls=%fused_computation.3.clone.1 | convolution fusion | flops 1090535424 | bytes 71311360 | tf_op jit(solution)/shard_map/while/body/eval_jaxpr/dot_general | solution.py:40
  259.7 24.6 %convolution_add_fusion.2 = f32[256,32768]{1,0:T(8,128)} fusion(bf16[64,32768]{1,0:T(8,128)(2,1)S(1)} %bitcast.29, f32[256,32768]{1,0:T(8,128)} %get-tuple-element.281, pred[]{:T(512)S(6)} %compare.3, pred[256,32]{0,1:T(32,128)(4,1)S(1)} %fusion.34), kind=kOutput, calls=%fused_computation.3.clone.1 | convolution fusion | flops 1090535424 | bytes 71311360 | tf_op jit(solution)/shard_map/while/body/eval_jaxpr/dot_general | solution.py:40
  295.2 24.6 %convolution_add_fusion.2 = f32[256,32768]{1,0:T(8,128)} fusion(bf16[64,32768]{1,0:T(8,128)(2,1)S(1)} %bitcast.29, f32[256,32768]{1,0:T(8,128)} %get-tuple-element.281, pred[]{:T(512)S(6)} %compare.3, pred[256,32]{0,1:T(32,128)(4,1)S(1)} %fusion.34), kind=kOutput, calls=%fused_computation.3.clone.1 | convolution fusion | flops 1090535424 | bytes 71311360 | tf_op jit(solution)/shard_map/while/body/eval_jaxpr/dot_general | solution.py:40
  330.7 24.6 %convolution_add_fusion.2 = f32[256,32768]{1,0:T(8,128)} fusion(bf16[64,32768]{1,0:T(8,128)(2,1)S(1)} %bitcast.29, f32[256,32768]{1,0:T(8,128)} %get-tuple-element.281, pred[]{:T(512)S(6)} %compare.3, pred[256,32]{0,1:T(32,128)(4,1)S(1)} %fusion.34), kind=kOutput, calls=%fused_computation.3.clone.1 | convolution fusion | flops 1090535424 | bytes 71311360 | tf_op jit(solution)/shard_map/while/body/eval_jaxpr/dot_general | solution.py:40
  366.2 24.6 %convolution_add_fusion.2 = f32[256,32768]{1,0:T(8,128)} fusion(bf16[64,32768]{1,0:T(8,128)(2,1)S(1)} %bitcast.29, f32[256,32768]{1,0:T(8,128)} %get-tuple-element.281, pred[]{:T(512)S(6)} %compare.3, pred[256,32]{0,1:T(32,128)(4,1)S(1)} %fusion.34), kind=kOutput, calls=%fused_computation.3.clone.1 | convolution fusion | flops 1090535424 | bytes 71311360 | tf_op jit(solution)/shard_map/while/body/eval_jaxpr/dot_general | solution.py:40
  391.7 4.6 convolution_convert_fusion.3
  401.7 24.6 %convolution_add_fusion.2 = f32[256,32768]{1,0:T(8,128)} fusion(bf16[64,32768]{1,0:T(8,128)(2,1)S(1)} %bitcast.29, f32[256,32768]{1,0:T(8,128)} %get-tuple-element.281, pred[]{:T(512)S(6)} %compare.3, pred[256,32]{0,1:T(32,128)(4,1)S(1)} %fusion.34), kind=kOutput, calls=%fused_computation.3.clone.1 | convolution fusion | flops 1090535424 | bytes 71311360 | tf_op jit(solution)/shard_map/while/body/eval_jaxpr/dot_general | solution.py:40
  427.2 4.6 convolution_convert_fusion.3
  437.2 24.6 %convolution_add_fusion.2 = f32[256,32768]{1,0:T(8,128)} fusion(bf16[64,32768]{1,0:T(8,128)(2,1)S(1)} %bitcast.29, f32[256,32768]{1,0:T(8,128)} %get-tuple-element.281, pred[]{:T(512)S(6)} %compare.3, pred[256,32]{0,1:T(32,128)(4,1)S(1)} %fusion.34), kind=kOutput, calls=%fused_computation.3.clone.1 | convolution fusion | flops 1090535424 | bytes 71311360 | tf_op jit(solution)/shard_map/while/body/eval_jaxpr/dot_general | solution.py:40
  461.8 17.1 %convert_element_type.45 = bf16[256,32768]{1,0:T(8,128)(2,1)} convert(f32[256,32768]{1,0:T(8,128)} %get-tuple-element.171) | non-fusion elementwise | flops 8388608 | bytes 50331648 | tf_op jit(solution)/shard_map/convert_element_type | solution.py:46
  478.9 25.6 %convert_element_type.46 = bf16[32768,256]{1,0:T(8,128)(2,1)} reshape(bf16[256,32768]{1,0:T(8,128)(2,1)} %convert_element_type.45) | data formatting | bytes 33554432 | tf_op jit(solution)/shard_map/convert_element_type | solution.py:46
  504.6 145.1 %reduce-scatter.2.cloned.1.call-done = bf16[2048,256]{1,0:T(8,128)(2,1)} async-done(((bf16[32768,256]{1,0:T(8,128)(2,1)}), bf16[2048,256]{1,0:T(8,128)(2,1)}) %reduce-scatter.2.cloned.1.call-update) | async-done | bytes 1048592 | tf_op jit(solution)/shard_map/reduce_scatter | solution.py:45
  652.1 136.6 %all-reduce.3.cloned.1.call-done = f32[256,256]{0,1:T(8,128)} async-done(((f32[256,256]{0,1:T(8,128)}), f32[256,256]{0,1:T(8,128)}) %all-reduce.3.cloned.1.call-update) | async-done | bytes 262160 | tf_op jit(solution)/shard_map/psum | solution.py:54
  791.5 69.7 %all-reduce.5.cloned.1.call-done = f32[256,256]{0,1:T(8,128)} async-done(((f32[256,256]{0,1:T(8,128)}), f32[256,256]{0,1:T(8,128)}) %all-reduce.5.cloned.1.call-update) | async-done | bytes 262160 | tf_op jit(solution)/shard_map/psum | solution.py:54
  (108 shorter events, 95.4 us)
Async XLA Ops:
  7.2 642.5 %copy-start = (bf16[2048,256]{1,0:T(8,128)(2,1)S(1)}, bf16[2048,256]{1,0:T(8,128)(2,1)}, u32[]{:S(2)}) copy-start(bf16[2048,256]{1,0:T(8,128)(2,1)} %param.12) | copy-start | bytes 3145732
  7.2 2.9 copy-start.2
  7.2 2.9 copy-start.3
  7.2 98.2 %all-gather.2.cloned.1.call-start = ((), (), s32[]{:S(2)}) async-start(), calls=%async_computation.1 | async-start | bytes 9437184 | tf_op jit(solution)/shard_map/all_gather | solution.py:11
  10.0 639.7 %reduce-scatter.2.cloned.1.call-start = ((), (), s32[]{:S(2)}) async-start(), calls=%async_computation.2 | async-start | bytes 17825792 | tf_op jit(solution)/shard_map/reduce_scatter | solution.py:45
  504.5 284.2 %copy-start.1 = (bf16[256,256]{1,0:T(8,128)(2,1)S(1)}, bf16[256,256]{1,0:T(8,128)(2,1)}, u32[]{:S(2)}) copy-start(bf16[256,256]{1,0:T(8,128)(2,1)} %param.13) | copy-start | bytes 393220
  504.6 284.2 %all-reduce.3.cloned.1.call-start = ((), (), s32[]{:S(2)}) async-start(), calls=%async_computation.3 | async-start | bytes 524288 | tf_op jit(solution)/shard_map/psum | solution.py:54
  652.1 209.0 %all-reduce.5.cloned.1.call-start = ((), (), s32[]{:S(2)}) async-start(), calls=%async_computation.4 | async-start | bytes 524288 | tf_op jit(solution)/shard_map/psum | solution.py:54
Sparse Core Ops, SparseCore 0:
  10.3 95.1 all-gather.1
  504.7 144.9 reduce-scatter.1
  652.9 135.8 all-reduce.2
  791.1 69.9 all-reduce.4
